TPU v7x, 32 devices: a whole 2x2x4 slice. The times are simulated.
32 devices in a mesh: groups: 2 (over y), win: 4 (over z), segment: 4 (over x, core).
Axes of the slice: x: 2, y: 2, z: 4, core: 2. Of those that a mesh axis runs over, the one named last changes fastest.
Arguments:
- fields: bfloat16 [8, 8, 64, 1536], P(('groups', 'segment'), None, 'win'), parts along dimension 0, may hold values from -12 to 12
- step_index: int32 [8], P(('groups', 'segment')), parts along dimension 0, may hold values from 0 to 31
- shift_flags: int32 [4], P('segment'), may hold values from 0 to 1, as said below
- norm_gains: float32 [4, 1536], P('segment'), may hold values from 0.5 to 2
- input_weight: bfloat16 [4, 1536, 2304], P('segment'), may hold values from -0.15625 to 0.15625
- output_weight: bfloat16 [4, 768, 1536], P('segment'), may hold values from -0.21875 to 0.21875
- step_table: float32 [32, 1536], replicated, may hold values from -6 to 6
- step_rate: float32 [32], replicated, may hold values from 0.25 to 1
Outputs:
- advanced: bfloat16 [8, 8, 64, 1536], P(('groups', 'segment'), None, 'win'), parts along dimension 0
There are 2 independent parts, one for each index of `groups`. A program takes and returns all parts, laid end to end along the dimension named above; an argument that names none is the same for every part. Nothing has to cross between parts.
Inputs may be any that keep to these rules, and one draw needn't show every extreme that they name: `shift_flags`: each entry is 0 or 1, and at least one layer has 1.
All inputs are finite; a program needn't handle non-finite values.
Results may differ from a plain program's by a relative error of at most 0.014.
Values may be sent and summed in bfloat16 or wider, within the bound.
A program may use at most 64 MiB of HBM per device.

v0:
```python
import functools
import math

import jax
import jax.numpy as jnp
from jax import lax
from jax.experimental import pallas as pl
from jax.experimental.pallas import tpu as pltpu
from jax.sharding import PartitionSpec as P

HEADS = 6
TILE = 256
MESH = pl.DeviceIdType.MESH


def pick(table, index):
    value = table[0]
    for at, entry in enumerate(table[1:], 1):
        value = jnp.where(index == at, entry, value)
    return value


def kernel(
    segments,
    windows,
    index_ref,
    flag_ref,
    rate_ref,
    fields_ref,
    table_ref,
    gain_ref,
    first_hbm,
    second_hbm,
    advanced_ref,
    first_weight,
    second_weight,
    start,
    inbox,
    outbox,
    returned,
    entry_relay,
    home_relay,
    normed,
    projected,
    heads,
    weight_sem,
    start_send,
    inbox_sem,
    outbox_sem,
    return_sem,
    entry_relay_recv,
    entry_relay_send,
    home_relay_recv,
    home_relay_send,
):
    seg = lax.axis_index("segment")
    win = lax.axis_index("win")
    stride = windows // segments
    working = lax.rem(win, stride) == 0
    spread = sorted(range(segments), key=lambda at: abs(2 * at + 1 - segments))
    column_of = [at * stride for at in spread]
    sample = pick([spread.index(at) for at in range(segments)], win // stride)
    lower = segments // 2

    def entry_relayed(owner, chunk):
        column = column_of[owner] if isinstance(owner, int) else pick(column_of, owner)
        return (owner >= lower) & (jnp.abs(chunk - column) == 1)

    def home_relayed(owner, column, chunk):
        return (owner < lower) & ((2 * chunk >= windows) != (2 * column >= windows))

    half_tokens = start.shape[0] // 2
    lat_rows, cols, width = fields_ref.shape
    half = cols // 2
    inner_width = second_weight.shape[0]
    head_size = inner_width // HEADS
    last_layer = seg == segments - 1

    first_copy = pltpu.make_async_copy(first_hbm, first_weight, weight_sem.at[0])
    second_copy = pltpu.make_async_copy(second_hbm, second_weight, weight_sem.at[1])

    @pl.when(working)
    def _():
        first_copy.start()
        second_copy.start()

    barrier = pltpu.get_barrier_semaphore()
    count = segments * windows
    me = seg * windows + win

    @pl.loop(1, count)
    def _(step):
        other = lax.rem(me + step, count)
        pl.semaphore_signal(
            barrier,
            inc=1,
            device_id={"segment": other // windows, "win": lax.rem(other, windows)},
            device_id_type=MESH,
        )

    step_index = index_ref[0]
    offset_row = table_ref[pl.ds(step_index, 1), :]
    for side in range(2):
        piece = fields_ref[:, side * half : (side + 1) * half, :].astype(jnp.float32)
        piece = piece.reshape(half_tokens, width) + offset_row
        start[side * half_tokens : (side + 1) * half_tokens, :] = piece.astype(jnp.bfloat16)

    pl.semaphore_wait(barrier, count - 1)

    entry = pick(column_of, seg)
    entry_by_relay = entry_relayed(seg, win)
    relays_home = working & (sample == seg) & (seg < lower)
    stays = (seg == 0) & (win == entry)
    goes_home = (seg == segments - 1) & working & (sample == seg)

    start_copy = pltpu.make_async_remote_copy(
        src_ref=start,
        dst_ref=inbox.at[win],
        send_sem=start_send,
        recv_sem=inbox_sem.at[win],
        device_id={"segment": 0, "win": entry},
        device_id_type=MESH,
    )

    @pl.when(stays)
    def _():
        inbox[win] = start[...]

    start_relay = pltpu.make_async_remote_copy(
        src_ref=start,
        dst_ref=entry_relay.at[jnp.maximum(seg - lower, 0)],
        send_sem=start_send,
        recv_sem=entry_relay_recv.at[jnp.maximum(seg - lower, 0)],
        device_id={"segment": 1},
        device_id_type=MESH,
    )

    @pl.when(entry_by_relay)
    def _():
        start_relay.start()

    @pl.when(jnp.logical_not(stays) & jnp.logical_not(entry_by_relay))
    def _():
        start_copy.start()

    def entry_forward(owner):
        return pltpu.make_async_remote_copy(
            src_ref=entry_relay.at[owner - lower],
            dst_ref=inbox.at[win],
            send_sem=entry_relay_send.at[owner - lower],
            recv_sem=inbox_sem.at[win],
            device_id={"segment": 0, "win": column_of[owner]},
            device_id_type=MESH,
        )

    for owner in range(lower, segments):

        @pl.when((seg == 1) & entry_relayed(owner, win))
        def _():
            pltpu.make_async_remote_copy(
                src_ref=start,
                dst_ref=entry_relay.at[owner - lower],
                send_sem=start_send,
                recv_sem=entry_relay_recv.at[owner - lower],
                device_id={"segment": 0},
                device_id_type=MESH,
            ).wait_recv()
            entry_forward(owner).start()

    def arrival(chunk):
        return pltpu.make_async_remote_copy(
            src_ref=start,
            dst_ref=inbox.at[chunk],
            send_sem=start_send,
            recv_sem=inbox_sem.at[chunk],
            device_id={"segment": 0, "win": entry},
            device_id_type=MESH,
        )

    def onward(chunk):
        return pltpu.make_async_remote_copy(
            src_ref=outbox.at[chunk],
            dst_ref=inbox.at[chunk],
            send_sem=outbox_sem.at[chunk],
            recv_sem=inbox_sem.at[chunk],
            device_id={"segment": lax.rem(seg + 1, segments)},
            device_id_type=MESH,
        )

    def homeward(chunk):
        return pltpu.make_async_remote_copy(
            src_ref=outbox.at[chunk],
            dst_ref=returned,
            send_sem=outbox_sem.at[chunk],
            recv_sem=return_sem,
            device_id={"segment": sample, "win": chunk},
            device_id_type=MESH,
        )

    def home_through(chunk):
        return pltpu.make_async_remote_copy(
            src_ref=outbox.at[chunk],
            dst_ref=home_relay.at[chunk],
            send_sem=outbox_sem.at[chunk],
            recv_sem=home_relay_recv.at[chunk],
            device_id={"segment": sample},
            device_id_type=MESH,
        )

    def home_forward(chunk):
        return pltpu.make_async_remote_copy(
            src_ref=home_relay.at[chunk],
            dst_ref=returned,
            send_sem=home_relay_send.at[chunk],
            recv_sem=return_sem,
            device_id={"win": chunk},
            device_id_type=MESH,
        )

    def await_chunk(chunk):
        @pl.when(jnp.logical_not(stays & (chunk == win)))
        def _():
            arrival(chunk).wait_recv()

    @pl.when(working)
    def _():
        shift = jnp.where(flag_ref[0] > 0, 1, 0)
        base = lax.rem(win + seg + 1, windows)
        halves = 2 * windows

        def project(chunk):
            gain_row = gain_ref[...]
            value = inbox[chunk].astype(jnp.float32)
            mean_square = jnp.mean(value * value, axis=-1, keepdims=True)
            scale = lax.rsqrt(mean_square + 1e-06)
            normed[...] = (value * gain_row).astype(jnp.bfloat16)
            for at in range(0, 3 * inner_width, TILE):
                part = jnp.dot(
                    normed[...], first_weight[:, at : at + TILE], preferred_element_type=jnp.float32
                )
                part = (part * scale).astype(jnp.bfloat16)
                projected[2 * chunk, :, at : at + TILE] = part[:half_tokens]
                projected[2 * chunk + 1, :, at : at + TILE] = part[half_tokens:]

        def attend(unit):
            left = 2 * unit + shift
            right = lax.rem(left + 1, halves)

            def block(at):
                part = pl.ds(at, head_size)
                return jnp.concatenate([projected[left, :, part], projected[right, :, part]], axis=0)

            starts = range(0, inner_width, head_size)
            scores = [
                lax.dot_general(
                    block(at),
                    block(inner_width + at),
                    (((1,), (1,)), ((), ())),
                    preferred_element_type=jnp.float32,
                )
                for at in starts
            ]
            weights = [jnp.exp(score * (1.0 / math.sqrt(head_size))) for score in scores]
            totals = [jnp.sum(weight, axis=-1, keepdims=True) for weight in weights]
            weights = [
                (weight * (1.0 / total)).astype(jnp.bfloat16)
                for weight, total in zip(weights, totals)
            ]
            mixed = [
                jnp.dot(
                    weight, block(2 * inner_width + at), preferred_element_type=jnp.float32
                ).astype(jnp.bfloat16)
                for weight, at in zip(weights, starts)
            ]
            for at, mix in zip(starts, mixed):
                heads[2 * unit, :, at : at + head_size] = mix[:half_tokens]
                heads[2 * unit + 1, :, at : at + head_size] = mix[half_tokens:]

        def emit(chunk):
            left = lax.rem(2 * chunk + halves - shift, halves)
            right = 2 * chunk + 1 - shift
            own = jnp.concatenate([heads[left], heads[right]], axis=0)
            for at in range(0, width, TILE):
                branch = jnp.dot(
                    own, second_weight[:, at : at + TILE], preferred_element_type=jnp.float32
                ).astype(jnp.bfloat16)
                outbox[chunk, :, at : at + TILE] = (
                    inbox[chunk, :, at : at + TILE].astype(jnp.float32) + branch.astype(jnp.float32)
                ).astype(jnp.bfloat16)

            @pl.when(jnp.logical_not(last_layer))
            def _():
                onward(chunk).start()

            through = home_relayed(sample, win, chunk)

            @pl.when(last_layer & through)
            def _():
                home_through(chunk).start()

            @pl.when(
                last_layer & jnp.logical_not(through) & jnp.logical_not(goes_home & (chunk == win))
            )
            def _():
                homeward(chunk).start()

            @pl.when(goes_home & (chunk == win))
            def _():
                returned[...] = outbox[chunk]

        first_copy.wait()
        second_copy.wait()

        @pl.loop(0, windows + 2)
        def _(step):
            chunk = lax.rem(base + step, windows)

            @pl.when(step < windows)
            def _():
                await_chunk(chunk)
                project(chunk)

            @pl.when((step > 0) & (step <= windows))
            def _():
                attend(lax.rem(chunk + windows - 1, windows))

            @pl.when(step > 1)
            def _():
                emit(lax.rem(chunk + windows - 1, windows))

    @pl.when(relays_home)
    def _():
        @pl.loop(0, windows)
        def _(step):
            chunk = lax.rem(win + segments + step, windows)

            @pl.when(home_relayed(seg, win, chunk))
            def _():
                home_through(chunk).wait_recv()
                home_forward(chunk).start()

    @pl.when(jnp.logical_not(goes_home))
    def _():
        homeward(win).wait_recv()

    rate = rate_ref[step_index]
    for side in range(2):
        fields_part = fields_ref[:, side * half : (side + 1) * half, :].astype(jnp.float32)
        rows = pl.ds(side * half_tokens, half_tokens)
        velocity = returned[rows, :].astype(jnp.float32) - start[rows, :].astype(jnp.float32)
        advanced_ref[:, side * half : (side + 1) * half, :] = (
            fields_part + rate * velocity.reshape(lat_rows, half, width)
        ).astype(jnp.bfloat16)

    @pl.when(jnp.logical_not(stays))
    def _():
        start_copy.wait_send()

    for owner in range(lower, segments):

        @pl.when((seg == 1) & entry_relayed(owner, win))
        def _():
            entry_forward(owner).wait_send()

    @pl.when(relays_home)
    def _():
        @pl.loop(0, windows)
        def _(chunk):
            @pl.when(home_relayed(seg, win, chunk))
            def _():
                home_forward(chunk).wait_send()

    @pl.when(working)
    def _():
        @pl.loop(0, windows)
        def _(chunk):
            @pl.when(jnp.logical_not(goes_home & (chunk == win)))
            def _():
                homeward(chunk).wait_send()


def shards(
    fields, step_index, shift_flags, norm_gains, input_weight, output_weight, step_table, step_rate
):
    segments, windows = lax.axis_size("segment"), lax.axis_size("win")
    _, lat_rows, cols, width = fields.shape
    tokens = lat_rows * cols
    inner_width = output_weight.shape[1]
    smem = pl.BlockSpec(memory_space=pltpu.SMEM)
    vmem = pl.BlockSpec(memory_space=pltpu.VMEM)
    hbm = pl.BlockSpec(memory_space=pl.ANY)
    advanced = pl.pallas_call(
        functools.partial(kernel, segments, windows),
        out_shape=jax.ShapeDtypeStruct((lat_rows, cols, width), jnp.bfloat16),
        in_specs=[smem, smem, smem, vmem, vmem, vmem, hbm, hbm],
        out_specs=vmem,
        scratch_shapes=[
            pltpu.VMEM(input_weight.shape[1:], jnp.bfloat16),
            pltpu.VMEM(output_weight.shape[1:], jnp.bfloat16),
            pltpu.VMEM((tokens, width), jnp.bfloat16),
            pltpu.VMEM((windows, tokens, width), jnp.bfloat16),
            pltpu.VMEM((windows, tokens, width), jnp.bfloat16),
            pltpu.VMEM((tokens, width), jnp.bfloat16),
            pltpu.VMEM((segments - segments // 2, tokens, width), jnp.bfloat16),
            pltpu.VMEM((windows, tokens, width), jnp.bfloat16),
            pltpu.VMEM((tokens, width), jnp.bfloat16),
            pltpu.VMEM((2 * windows, tokens // 2, 3 * inner_width), jnp.bfloat16),
            pltpu.VMEM((2 * windows, tokens // 2, inner_width), jnp.bfloat16),
            pltpu.SemaphoreType.DMA((2,)),
            pltpu.SemaphoreType.DMA,
            pltpu.SemaphoreType.DMA((windows,)),
            pltpu.SemaphoreType.DMA((windows,)),
            pltpu.SemaphoreType.DMA,
            pltpu.SemaphoreType.DMA((segments - segments // 2,)),
            pltpu.SemaphoreType.DMA((segments - segments // 2,)),
            pltpu.SemaphoreType.DMA((windows,)),
            pltpu.SemaphoreType.DMA((windows,)),
        ],
        compiler_params=pltpu.CompilerParams(
            collective_id=0, has_side_effects=True, vmem_limit_bytes=60 * 1024 * 1024
        ),
    )(
        step_index,
        shift_flags,
        step_rate,
        fields[0],
        step_table,
        norm_gains,
        input_weight[0],
        output_weight[0],
    )
    return advanced[None]


def solution(mesh):
    return jax.shard_map(
        shards,
        mesh=mesh,
        in_specs=(
            P(("groups", "segment"), None, "win", None),
            P(("groups", "segment")),
            P("segment"),
            P("segment", None),
            P("segment", None, None),
            P("segment", None, None),
            P(),
            P(),
        ),
        out_specs=P(("groups", "segment"), None, "win", None),
        check_vma=False,
    )
```

profile of v0, /device:TPU:13, one launch (start us, length us, event | category | flops | bytes accessed | tf_op | source)
XLA Modules:
  0.0 75.8 jit_solution(9157723892206726426)
XLA Ops:
  1.3 72.7 %shard_map.82 = bf16[8,16,1536]{2,1,0:T(8,128)(2,1)} custom-call(s32[1]{0:T(128)S(6)} %copy.10.index_ref, s32[1]{0:T(128)S(6)} %copy.11.flag_ref, f32[32]{0:T(128)} %rate_ref.1, bf16[8,16,1536]{2,1,0:T(8,128)(2,1)} %bitcast.7, f32[32,1536]{1,0:T(8,128)} %table_ref.1, f32[1,1536]{1,0:T(1,128)} %gain_ref.1, bf16[1536,2304]{1,0:T(8,128)(2,1)} %bitcast.4, ...), custom_call_target="tpu_custom_call" | custom-call | tf_op jit(solution)/shard_map/pallas_call | solution.py:392
  74.0 1.8 %copy.12 = bf16[1,8,16,1536]{3,2,1,0:T(8,128)(2,1)} copy(bf16[1,8,16,1536]{3,2,1,0:T(8,128)(2,1)} %bitcast.6) | data formatting | bytes 786432
where the time goes:
time: 76 us; the launch traced here: 75.8 us
  Pallas kernels  72.7 us (96%)
  local copies, waits for them, and re-layouts  1.77 us (2%)
  between operations  1.3 us (2%)
    pallas_call x1, Pallas kernels, shards(): pl.pallas_call(functools.partial(kernel, segments, windows), out_shape=ja...  72.7 us
    unnamed x1, local copies, waits for them, and re-layouts  1.77 us

commit v1 on v0

--- a/solution.py
+++ b/solution.py
@@ -52,6 +52,7 @@
     entry_relay_send,
     home_relay_recv,
     home_relay_send,
+    turn,
 ):
     seg = lax.axis_index("segment")
     win = lax.axis_index("win")
@@ -59,12 +60,31 @@
     working = lax.rem(win, stride) == 0
     spread = sorted(range(segments), key=lambda at: abs(2 * at + 1 - segments))
     column_of = [at * stride for at in spread]
+    lower = segments // 2
+    step_of = [
+        1 if (2 * column + 1 > windows) == (owner >= lower) else -1
+        for owner, column in enumerate(column_of)
+    ]
     sample = pick([spread.index(at) for at in range(segments)], win // stride)
-    lower = segments // 2
+
+    def place(owner):
+        if isinstance(owner, int):
+            return column_of[owner], step_of[owner]
+        return pick(column_of, owner), pick(step_of, owner)
+
+    def slot_of(owner, chunk):
+        column, step = place(owner)
+        return lax.rem(step * (chunk - column) + 1 + 2 * windows, windows)
+
+    def home_chunk(owner, slot):
+        column, step = place(owner)
+        turns = lax.rem(slot + segments // 2 - 1 + windows, windows)
+        return lax.rem(column + step * turns + windows, windows)
 
     def entry_relayed(owner, chunk):
-        column = column_of[owner] if isinstance(owner, int) else pick(column_of, owner)
-        return (owner >= lower) & (jnp.abs(chunk - column) == 1)
+        column, _ = place(owner)
+        distance = jnp.abs(chunk - column)
+        return (owner >= lower) & (distance > 0) & (2 * distance <= windows)
 
     def home_relayed(owner, column, chunk):
         return (owner < lower) & ((2 * chunk >= windows) != (2 * column >= windows))
@@ -98,33 +118,44 @@
             device_id_type=MESH,
         )
 
+    entry, step_here = place(seg)
+
+    def columns(side):
+        at = jnp.where(step_here > 0, side * half, (1 - side) * half)
+        return pl.ds(pl.multiple_of(at, half), half)
+
     step_index = index_ref[0]
     offset_row = table_ref[pl.ds(step_index, 1), :]
     for side in range(2):
-        piece = fields_ref[:, side * half : (side + 1) * half, :].astype(jnp.float32)
+        piece = fields_ref[:, columns(side), :].astype(jnp.float32)
         piece = piece.reshape(half_tokens, width) + offset_row
         start[side * half_tokens : (side + 1) * half_tokens, :] = piece.astype(jnp.bfloat16)
 
     pl.semaphore_wait(barrier, count - 1)
 
-    entry = pick(column_of, seg)
+    entry_slot = slot_of(seg, win)
     entry_by_relay = entry_relayed(seg, win)
     relays_home = working & (sample == seg) & (seg < lower)
     stays = (seg == 0) & (win == entry)
     goes_home = (seg == segments - 1) & working & (sample == seg)
 
+    pair = seg + 1 - 2 * lax.rem(seg, 2)
+    lead = slot_of(pair, win) - entry_slot
+    gives = 2 * lead > windows
+    yields = -2 * lead > windows
+
     start_copy = pltpu.make_async_remote_copy(
         src_ref=start,
-        dst_ref=inbox.at[win],
+        dst_ref=inbox.at[entry_slot],
         send_sem=start_send,
-        recv_sem=inbox_sem.at[win],
+        recv_sem=inbox_sem.at[entry_slot],
         device_id={"segment": 0, "win": entry},
         device_id_type=MESH,
     )
 
     @pl.when(stays)
     def _():
-        inbox[win] = start[...]
+        inbox[entry_slot] = start[...]
 
     start_relay = pltpu.make_async_remote_copy(
         src_ref=start,
@@ -135,6 +166,10 @@
         device_id_type=MESH,
     )
 
+    @pl.when(yields)
+    def _():
+        pl.semaphore_wait(turn, 1)
+
     @pl.when(entry_by_relay)
     def _():
         start_relay.start()
@@ -143,18 +178,26 @@
     def _():
         start_copy.start()
 
+    @pl.when(gives)
+    def _():
+        @pl.when(jnp.logical_not(stays))
+        def _():
+            start_copy.wait_send()
+
+        pl.semaphore_signal(turn, inc=1, device_id={"segment": pair}, device_id_type=MESH)
+
     def entry_forward(owner):
+        slot = slot_of(owner, win)
         return pltpu.make_async_remote_copy(
             src_ref=entry_relay.at[owner - lower],
-            dst_ref=inbox.at[win],
+            dst_ref=inbox.at[slot],
             send_sem=entry_relay_send.at[owner - lower],
-            recv_sem=inbox_sem.at[win],
+            recv_sem=inbox_sem.at[slot],
             device_id={"segment": 0, "win": column_of[owner]},
             device_id_type=MESH,
         )
 
-    for owner in range(lower, segments):
-
+    def entry_pass(owner):
         @pl.when((seg == 1) & entry_relayed(owner, win))
         def _():
             pltpu.make_async_remote_copy(
@@ -167,70 +210,77 @@
             ).wait_recv()
             entry_forward(owner).start()
 
-    def arrival(chunk):
+    low_half = 2 * win < windows
+
+    @pl.when(low_half)
+    def _():
+        for owner in sorted(range(lower, segments), key=lambda at: column_of[at]):
+            entry_pass(owner)
+
+    @pl.when(jnp.logical_not(low_half))
+    def _():
+        for owner in sorted(range(lower, segments), key=lambda at: -column_of[at]):
+            entry_pass(owner)
+
+    def arrival(slot):
         return pltpu.make_async_remote_copy(
             src_ref=start,
-            dst_ref=inbox.at[chunk],
+            dst_ref=inbox.at[slot],
             send_sem=start_send,
-            recv_sem=inbox_sem.at[chunk],
+            recv_sem=inbox_sem.at[slot],
             device_id={"segment": 0, "win": entry},
             device_id_type=MESH,
         )
 
-    def onward(chunk):
+    def onward(slot):
         return pltpu.make_async_remote_copy(
-            src_ref=outbox.at[chunk],
-            dst_ref=inbox.at[chunk],
-            send_sem=outbox_sem.at[chunk],
-            recv_sem=inbox_sem.at[chunk],
+            src_ref=outbox.at[slot],
+            dst_ref=inbox.at[slot],
+            send_sem=outbox_sem.at[slot],
+            recv_sem=inbox_sem.at[slot],
             device_id={"segment": lax.rem(seg + 1, segments)},
             device_id_type=MESH,
         )
 
-    def homeward(chunk):
+    def homeward(slot):
         return pltpu.make_async_remote_copy(
-            src_ref=outbox.at[chunk],
+            src_ref=outbox.at[slot],
             dst_ref=returned,
-            send_sem=outbox_sem.at[chunk],
+            send_sem=outbox_sem.at[slot],
             recv_sem=return_sem,
-            device_id={"segment": sample, "win": chunk},
-            device_id_type=MESH,
-        )
-
-    def home_through(chunk):
+            device_id={"segment": sample, "win": home_chunk(sample, slot)},
+            device_id_type=MESH,
+        )
+
+    def home_through(slot):
         return pltpu.make_async_remote_copy(
-            src_ref=outbox.at[chunk],
-            dst_ref=home_relay.at[chunk],
-            send_sem=outbox_sem.at[chunk],
-            recv_sem=home_relay_recv.at[chunk],
+            src_ref=outbox.at[slot],
+            dst_ref=home_relay.at[slot],
+            send_sem=outbox_sem.at[slot],
+            recv_sem=home_relay_recv.at[slot],
             device_id={"segment": sample},
             device_id_type=MESH,
         )
 
-    def home_forward(chunk):
+    def home_forward(slot):
         return pltpu.make_async_remote_copy(
-            src_ref=home_relay.at[chunk],
+            src_ref=home_relay.at[slot],
             dst_ref=returned,
-            send_sem=home_relay_send.at[chunk],
+            send_sem=home_relay_send.at[slot],
             recv_sem=return_sem,
-            device_id={"win": chunk},
-            device_id_type=MESH,
-        )
-
-    def await_chunk(chunk):
-        @pl.when(jnp.logical_not(stays & (chunk == win)))
-        def _():
-            arrival(chunk).wait_recv()
+            device_id={"win": home_chunk(sample, slot)},
+            device_id_type=MESH,
+        )
 
     @pl.when(working)
     def _():
         shift = jnp.where(flag_ref[0] > 0, 1, 0)
-        base = lax.rem(win + seg + 1, windows)
+        straddle = jnp.where(lax.rem(seg, 2) == 0, shift, 1 - shift)
         halves = 2 * windows
 
-        def project(chunk):
+        def project(slot):
             gain_row = gain_ref[...]
-            value = inbox[chunk].astype(jnp.float32)
+            value = inbox[slot].astype(jnp.float32)
             mean_square = jnp.mean(value * value, axis=-1, keepdims=True)
             scale = lax.rsqrt(mean_square + 1e-06)
             normed[...] = (value * gain_row).astype(jnp.bfloat16)
@@ -239,11 +289,11 @@
                     normed[...], first_weight[:, at : at + TILE], preferred_element_type=jnp.float32
                 )
                 part = (part * scale).astype(jnp.bfloat16)
-                projected[2 * chunk, :, at : at + TILE] = part[:half_tokens]
-                projected[2 * chunk + 1, :, at : at + TILE] = part[half_tokens:]
+                projected[2 * slot, :, at : at + TILE] = part[:half_tokens]
+                projected[2 * slot + 1, :, at : at + TILE] = part[half_tokens:]
 
         def attend(unit):
-            left = 2 * unit + shift
+            left = jnp.where(unit == 0, 0, lax.rem(2 * unit + halves - straddle, halves))
             right = lax.rem(left + 1, halves)
 
             def block(at):
@@ -276,83 +326,88 @@
                 heads[2 * unit, :, at : at + head_size] = mix[:half_tokens]
                 heads[2 * unit + 1, :, at : at + head_size] = mix[half_tokens:]
 
-        def emit(chunk):
-            left = lax.rem(2 * chunk + halves - shift, halves)
-            right = 2 * chunk + 1 - shift
-            own = jnp.concatenate([heads[left], heads[right]], axis=0)
+        def emit(slot):
+            later = lax.rem(slot + 1, windows)
+            first = 2 * slot + 1 + straddle
+            own = jnp.concatenate([heads[first], heads[first + 1]], axis=0)
             for at in range(0, width, TILE):
                 branch = jnp.dot(
                     own, second_weight[:, at : at + TILE], preferred_element_type=jnp.float32
                 ).astype(jnp.bfloat16)
-                outbox[chunk, :, at : at + TILE] = (
-                    inbox[chunk, :, at : at + TILE].astype(jnp.float32) + branch.astype(jnp.float32)
+                hidden = jnp.concatenate(
+                    [
+                        inbox[slot, half_tokens:, at : at + TILE],
+                        inbox[later, :half_tokens, at : at + TILE],
+                    ],
+                    axis=0,
+                )
+                outbox[slot, :, at : at + TILE] = (
+                    hidden.astype(jnp.float32) + branch.astype(jnp.float32)
                 ).astype(jnp.bfloat16)
 
             @pl.when(jnp.logical_not(last_layer))
             def _():
-                onward(chunk).start()
-
+                onward(slot).start()
+
+            chunk = home_chunk(sample, slot)
             through = home_relayed(sample, win, chunk)
 
             @pl.when(last_layer & through)
             def _():
-                home_through(chunk).start()
+                home_through(slot).start()
 
             @pl.when(
                 last_layer & jnp.logical_not(through) & jnp.logical_not(goes_home & (chunk == win))
             )
             def _():
-                homeward(chunk).start()
+                homeward(slot).start()
 
             @pl.when(goes_home & (chunk == win))
             def _():
-                returned[...] = outbox[chunk]
+                returned[...] = outbox[slot]
 
         first_copy.wait()
         second_copy.wait()
 
-        @pl.loop(0, windows + 2)
+        @pl.loop(0, windows + 1)
         def _(step):
-            chunk = lax.rem(base + step, windows)
-
             @pl.when(step < windows)
             def _():
-                await_chunk(chunk)
-                project(chunk)
-
-            @pl.when((step > 0) & (step <= windows))
-            def _():
-                attend(lax.rem(chunk + windows - 1, windows))
-
-            @pl.when(step > 1)
-            def _():
-                emit(lax.rem(chunk + windows - 1, windows))
+                @pl.when(jnp.logical_not(stays & (step == entry_slot)))
+                def _():
+                    arrival(step).wait_recv()
+
+                project(step)
+
+            attend(step)
+
+            @pl.when(step > 0)
+            def _():
+                emit(step - 1)
 
     @pl.when(relays_home)
     def _():
         @pl.loop(0, windows)
-        def _(step):
-            chunk = lax.rem(win + segments + step, windows)
-
-            @pl.when(home_relayed(seg, win, chunk))
-            def _():
-                home_through(chunk).wait_recv()
-                home_forward(chunk).start()
+        def _(slot):
+            @pl.when(home_relayed(seg, win, home_chunk(sample, slot)))
+            def _():
+                home_through(slot).wait_recv()
+                home_forward(slot).start()
 
     @pl.when(jnp.logical_not(goes_home))
     def _():
-        homeward(win).wait_recv()
+        homeward(0).wait_recv()
 
     rate = rate_ref[step_index]
     for side in range(2):
-        fields_part = fields_ref[:, side * half : (side + 1) * half, :].astype(jnp.float32)
+        fields_part = fields_ref[:, columns(side), :].astype(jnp.float32)
         rows = pl.ds(side * half_tokens, half_tokens)
         velocity = returned[rows, :].astype(jnp.float32) - start[rows, :].astype(jnp.float32)
-        advanced_ref[:, side * half : (side + 1) * half, :] = (
+        advanced_ref[:, columns(side), :] = (
             fields_part + rate * velocity.reshape(lat_rows, half, width)
         ).astype(jnp.bfloat16)
 
-    @pl.when(jnp.logical_not(stays))
+    @pl.when(jnp.logical_not(stays) & jnp.logical_not(gives))
     def _():
         start_copy.wait_send()
 
@@ -365,18 +420,18 @@
     @pl.when(relays_home)
     def _():
         @pl.loop(0, windows)
-        def _(chunk):
-            @pl.when(home_relayed(seg, win, chunk))
-            def _():
-                home_forward(chunk).wait_send()
+        def _(slot):
+            @pl.when(home_relayed(seg, win, home_chunk(sample, slot)))
+            def _():
+                home_forward(slot).wait_send()
 
     @pl.when(working)
     def _():
         @pl.loop(0, windows)
-        def _(chunk):
-            @pl.when(jnp.logical_not(goes_home & (chunk == win)))
-            def _():
-                homeward(chunk).wait_send()
+        def _(slot):
+            @pl.when(jnp.logical_not(goes_home & (home_chunk(sample, slot) == win)))
+            def _():
+                homeward(slot).wait_send()
 
 
 def shards(
@@ -405,7 +460,7 @@
             pltpu.VMEM((windows, tokens, width), jnp.bfloat16),
             pltpu.VMEM((tokens, width), jnp.bfloat16),
             pltpu.VMEM((2 * windows, tokens // 2, 3 * inner_width), jnp.bfloat16),
-            pltpu.VMEM((2 * windows, tokens // 2, inner_width), jnp.bfloat16),
+            pltpu.VMEM((2 * windows + 2, tokens // 2, inner_width), jnp.bfloat16),
             pltpu.SemaphoreType.DMA((2,)),
             pltpu.SemaphoreType.DMA,
             pltpu.SemaphoreType.DMA((windows,)),
@@ -415,6 +470,7 @@
             pltpu.SemaphoreType.DMA((segments - segments // 2,)),
             pltpu.SemaphoreType.DMA((windows,)),
             pltpu.SemaphoreType.DMA((windows,)),
+            pltpu.SemaphoreType.REGULAR,
         ],
         compiler_params=pltpu.CompilerParams(
             collective_id=0, has_side_effects=True, vmem_limit_bytes=60 * 1024 * 1024

time: 76 us -> 65.7 us (0.86)
  the two profiles are of different devices: /device:TPU:13 before, /device:TPU:14 now
where the time goes in v1:
time: 65.7 us; the launch traced here: 65.5 us
  Pallas kernels  62.5 us (95%)
  local copies, waits for them, and re-layouts  1.77 us (3%)
  between operations  1.3 us (2%)
    pallas_call x1, Pallas kernels, shards(): pl.pallas_call(functools.partial(kernel, segments, windows), out_shape=ja...  62.5 us
    unnamed x1, local copies, waits for them, and re-layouts  1.77 us

profile of v1, /device:TPU:14, one launch (start us, length us, event | category | flops | bytes accessed | tf_op | source)
XLA Modules:
  0.0 65.5 jit_solution(5255479702254095689)
XLA Ops:
  1.3 62.5 %shard_map.82 = bf16[8,16,1536]{2,1,0:T(8,128)(2,1)} custom-call(s32[1]{0:T(128)S(6)} %copy.10.index_ref, s32[1]{0:T(128)S(6)} %copy.11.flag_ref, f32[32]{0:T(128)} %rate_ref.1, bf16[8,16,1536]{2,1,0:T(8,128)(2,1)} %bitcast.7, f32[32,1536]{1,0:T(8,128)} %table_ref.1, f32[1,1536]{1,0:T(1,128)} %gain_ref.1, bf16[1536,2304]{1,0:T(8,128)(2,1)} %bitcast.4, ...), custom_call_target="tpu_custom_call" | custom-call | tf_op jit(solution)/shard_map/pallas_call | solution.py:447
  63.8 1.8 %copy.12 = bf16[1,8,16,1536]{3,2,1,0:T(8,128)(2,1)} copy(bf16[1,8,16,1536]{3,2,1,0:T(8,128)(2,1)} %bitcast.6) | data formatting | bytes 786432
